TPU v7x, 128 devices: a whole 4x4x4 slice. The times are simulated.
128 devices in a mesh: dp: 32 (over x, y, core), tensor: 4 (over z).
Axes of the slice: x: 4, y: 4, z: 4, core: 2. Of those that a mesh axis runs over, the one named last changes fastest.
Arguments:
- activations: bfloat16 [65536, 8192], P('dp', 'tensor'), may hold values from -16 to 16
- whitening: bfloat16 [8192, 1024], P('tensor'), may hold values from -8 to 8
- factor: bfloat16 [1024, 1024], P(('dp', 'tensor')), may hold values from -2 to 2
Outputs:
- new_factor: float32 [1024, 1024], P(('dp', 'tensor'))
All inputs are finite; a program needn't handle non-finite values.
Results may differ from a plain program's by a relative error of at most 0.029.
Values may be sent and summed in bfloat16 or wider, within the bound.
A program may use at most 192 MiB of HBM per device.

v0:
```python
import jax
import jax.numpy as jnp
from jax import lax
from jax.sharding import PartitionSpec as P

ridge_shift = 0.1
epsilon = 1e-06


def solve_rows(moment_rows, hadamard):
    lower = jnp.linalg.cholesky(hadamard)
    first = jax.scipy.linalg.solve_triangular(lower, moment_rows.T, lower=True)
    second = jax.scipy.linalg.solve_triangular(lower, first, lower=True, trans=1)
    return second.T


def shards(activations, whitening, factor):
    summed = lax.psum_scatter(
        jnp.dot(activations, whitening, preferred_element_type=jnp.float32).astype(jnp.bfloat16),
        "tensor",
        scatter_dimension=0,
        tiled=True,
    )
    whole_factor = lax.all_gather(factor, ("dp", "tensor"), axis=0, tiled=True)
    projected = jnp.dot(summed, whole_factor, preferred_element_type=jnp.float32)
    squared = (projected * projected).astype(jnp.bfloat16)
    moment_rows = lax.psum_scatter(
        lax.dot_general(
            summed, squared, (((0,), (0,)), ((), ())), preferred_element_type=jnp.float32
        ),
        ("dp", "tensor"),
        scatter_dimension=0,
        tiled=True,
    )
    gram = jnp.dot(whole_factor.T, whole_factor, preferred_element_type=jnp.float32)
    hadamard = gram * gram + ridge_shift * jnp.eye(gram.shape[0], dtype=jnp.float32)
    updated = solve_rows(moment_rows, hadamard)
    column_total = lax.psum(jnp.sum(updated * updated, axis=0), ("dp", "tensor"))
    scale = jnp.sqrt(column_total / whole_factor.shape[0] + epsilon)
    return updated / scale[None, :]


def solution(mesh):
    placed = (P("dp", "tensor"), P("tensor", None), P(("dp", "tensor"), None))
    return jax.shard_map(
        shards, mesh=mesh, in_specs=placed, out_specs=P(("dp", "tensor"), None), check_vma=False
    )
```

profile of v0, /device:TPU:1, one launch (start us, length us, event | category | flops | bytes accessed | tf_op | source)
XLA Modules:
  0.0 901.7 jit_solution(2923321162316526728)
XLA Ops:
  8.1 13.8 %convolution_convert_fusion = bf16[2048,1024]{1,0:T(8,128)(2,1)} fusion(bf16[2048,2048]{1,0:T(8,128)(2,1)} %param.3, bf16[2048,1024]{1,0:T(8,128)(2,1)} %param.4), kind=kOutput, calls=%fused_computation.8 | convolution fusion | flops 8592031744 | bytes 16777216 | tf_op jit(solution)/shard_map/dot_general | solution.py:19
  22.0 77.6 %all-gather.2.cloned.1.call-done = bf16[1024,1024]{1,0:T(8,128)(2,1)} async-done(((bf16[8,1024]{1,0:T(8,128)(2,1)}), bf16[1024,1024]{1,0:T(8,128)(2,1)}) %all-gather.2.cloned.1.call-update) | async-done | bytes 2097168 | tf_op jit(solution)/shard_map/all_gather | solution.py:24
  99.6 4.6 fusion.95
  104.3 2.0 copy-done
  106.2 2.4 multiply_bitcast_fusion
  108.6 5.8 copy.4
  114.4 4.5 add_multiply_fusion
  118.9 2.0 copy-done.1
  120.9 11.7 %cholesky.222 = f32[128,128]{1,0:T(8,128)S(1)} custom-call(f32[128,128]{1,0:T(8,128)S(1)} %cholesky.577), custom_call_target="Cholesky" | custom-call | tf_op jit(solution)/shard_map/jit(cholesky)/cholesky | solution.py:11
  132.6 2.5 cholesky.254
  135.1 9.8 %custom-call.66 = f32[1,128,128]{1,2,0:T(8,128)S(1)} custom-call(f32[1,128,128]{2,1,0:T(8,128)S(1)} %get-tuple-element.44), custom_call_target="InvertDiagBlocksLowerTriangular" | custom-call | tf_op jit(solution)/shard_map/jit(cholesky)/cholesky | solution.py:11
  144.9 2.3 constant_dynamic-update-slice_fusion.50
  147.3 1.5 convolution_subtract_fusion
  148.8 11.8 %cholesky.243 = f32[128,128]{1,0:T(8,128)S(1)} custom-call(f32[128,128]{1,0:T(8,128)S(1)} %cholesky.581), custom_call_target="Cholesky" | custom-call | tf_op jit(solution)/shard_map/jit(cholesky)/cholesky | solution.py:11
  160.7 5.9 fusion.1
  167.3 9.8 %custom-call.67 = f32[1,128,128]{1,2,0:T(8,128)S(1)} custom-call(f32[1,128,128]{2,1,0:T(8,128)S(1)} %get-tuple-element.41), custom_call_target="InvertDiagBlocksLowerTriangular" | custom-call | tf_op jit(solution)/shard_map/jit(cholesky)/cholesky | solution.py:11
  177.1 1.2 convolution_dynamic-update-slice_fusion
  178.3 2.1 convolution_subtract_fusion.1
  180.4 11.7 %cholesky.466 = f32[128,128]{1,0:T(8,128)S(1)} custom-call(f32[128,128]{1,0:T(8,128)S(1)} %cholesky.586), custom_call_target="Cholesky" | custom-call | tf_op jit(solution)/shard_map/jit(cholesky)/cholesky | solution.py:11
  192.8 9.8 %custom-call.68 = f32[1,128,128]{1,2,0:T(8,128)S(1)} custom-call(f32[1,128,128]{2,1,0:T(8,128)S(1)} %get-tuple-element.38), custom_call_target="InvertDiagBlocksLowerTriangular" | custom-call | tf_op jit(solution)/shard_map/jit(cholesky)/cholesky | solution.py:11
  202.6 1.2 convolution_dynamic-update-slice_fusion.1
  203.8 2.5 convolution_subtract_fusion.2
  206.3 11.7 %cholesky.485 = f32[128,128]{1,0:T(8,128)S(1)} custom-call(f32[128,128]{1,0:T(8,128)S(1)} %cholesky.591), custom_call_target="Cholesky" | custom-call | tf_op jit(solution)/shard_map/jit(cholesky)/cholesky | solution.py:11
  218.7 9.8 %custom-call.69 = f32[1,128,128]{1,2,0:T(8,128)S(1)} custom-call(f32[1,128,128]{2,1,0:T(8,128)S(1)} %get-tuple-element.35), custom_call_target="InvertDiagBlocksLowerTriangular" | custom-call | tf_op jit(solution)/shard_map/jit(cholesky)/cholesky | solution.py:11
  228.5 1.1 convolution_dynamic-update-slice_fusion.2
  229.6 2.4 convolution_subtract_fusion.3
  232.0 11.7 %cholesky.504 = f32[128,128]{1,0:T(8,128)S(1)} custom-call(f32[128,128]{1,0:T(8,128)S(1)} %cholesky.596), custom_call_target="Cholesky" | custom-call | tf_op jit(solution)/shard_map/jit(cholesky)/cholesky | solution.py:11
  244.4 10.2 %custom-call.70 = f32[1,128,128]{1,2,0:T(8,128)S(1)} custom-call(f32[1,128,128]{2,1,0:T(8,128)S(1)} %get-tuple-element.32), custom_call_target="InvertDiagBlocksLowerTriangular" | custom-call | tf_op jit(solution)/shard_map/jit(cholesky)/cholesky | solution.py:11
  254.6 1.0 convolution_dynamic-update-slice_fusion.3
  255.6 2.3 convolution_subtract_fusion.4
  257.9 11.7 %cholesky.524 = f32[128,128]{1,0:T(8,128)S(1)} custom-call(f32[128,128]{1,0:T(8,128)S(1)} %cholesky.601), custom_call_target="Cholesky" | custom-call | tf_op jit(solution)/shard_map/jit(cholesky)/cholesky | solution.py:11
  270.2 9.8 %custom-call.71 = f32[1,128,128]{1,2,0:T(8,128)S(1)} custom-call(f32[1,128,128]{2,1,0:T(8,128)S(1)} %get-tuple-element.29), custom_call_target="InvertDiagBlocksLowerTriangular" | custom-call | tf_op jit(solution)/shard_map/jit(cholesky)/cholesky | solution.py:11
  281.0 2.0 convolution_subtract_fusion.5
  283.0 11.9 %cholesky.544 = f32[128,128]{1,0:T(8,128)S(1)} custom-call(f32[128,128]{1,0:T(8,128)S(1)} %cholesky.606), custom_call_target="Cholesky" | custom-call | tf_op jit(solution)/shard_map/jit(cholesky)/cholesky | solution.py:11
  295.5 9.8 %custom-call.72 = f32[1,128,128]{1,2,0:T(8,128)S(1)} custom-call(f32[1,128,128]{2,1,0:T(8,128)S(1)} %get-tuple-element.26), custom_call_target="InvertDiagBlocksLowerTriangular" | custom-call | tf_op jit(solution)/shard_map/jit(cholesky)/cholesky | solution.py:11
  306.2 1.8 convolution_subtract_fusion.6
  308.0 11.7 %cholesky.562 = f32[128,128]{1,0:T(8,128)S(1)} custom-call(f32[128,128]{1,0:T(8,128)S(1)} %convolution_subtract_fusion.6), custom_call_target="Cholesky" | custom-call | tf_op jit(solution)/shard_map/jit(cholesky)/cholesky | solution.py:11
  329.9 4.8 select_select_fusion
  334.7 22.5 %while.1 = (s32[]{:T(128)}, f32[1024,1024]{1,0:T(8,128)}, s32[8,2]{0,1:T(2,128)S(1)}, f32[8,128,128]{2,1,0:T(8,128)S(1)}, s32[]{:T(128)}) while((s32[]{:T(128)}, f32[1024,1024]{1,0:T(8,128)}, s32[8,2]{0,1:T(2,128)S(1)}, f32[8,128,128]{2,1,0:T(8,128)S(1)}, s32[]{:T(128)}) %tuple.56), condition=%wide.while_cond, body=%wide.while_body.sunk | while | flops 2 | bytes 131189 | solution.py:13
  335.3 2.2 bitcast_dynamic-update-slice_fusion.2
  338.1 2.2 bitcast_dynamic-update-slice_fusion.2
  340.9 2.2 bitcast_dynamic-update-slice_fusion.2
  343.8 2.2 bitcast_dynamic-update-slice_fusion.2
  346.6 2.2 bitcast_dynamic-update-slice_fusion.2
  349.4 2.2 bitcast_dynamic-update-slice_fusion.2
  352.2 2.2 bitcast_dynamic-update-slice_fusion.2
  355.0 2.1 bitcast_dynamic-update-slice_fusion.2
  357.2 78.8 %custom-call.73 = f32[8,128,128]{1,2,0:T(8,128)S(1)} custom-call(f32[8,128,128]{2,1,0:T(8,128)S(1)} %get-tuple-element.12), custom_call_target="InvertDiagBlocksLowerTriangular" | custom-call | tf_op jit(solution)/shard_map/jit(_solve_triangular)/triangular_solve | solution.py:13
  436.0 365.3 %reduce-scatter.5.cloned.1.call-done = f32[8,1024]{1,0:T(8,128)} async-done(((f32[1024,1024]{1,0:T(8,128)}), f32[8,1024]{1,0:T(8,128)}) %reduce-scatter.5.cloned.1.call-update) | async-done | bytes 32784 | tf_op jit(solution)/shard_map/reduce_scatter | solution.py:27
  802.1 1.0 convolution_subtract_fusion.16
  803.3 1.1 convolution_subtract_fusion.15
  804.6 1.2 convolution_subtract_fusion.14
  806.0 1.2 convolution_subtract_fusion.13
  807.5 1.4 convolution_subtract_fusion.12
  809.1 1.4 convolution_subtract_fusion.20
  810.6 1.5 convolution_subtract_fusion.19
  812.7 1.0 convolution_subtract_fusion.11
  814.0 1.1 convolution_subtract_fusion.10
  815.3 1.2 convolution_subtract_fusion.9
  816.7 1.2 convolution_subtract_fusion.8
  818.2 1.3 convolution_subtract_fusion.7
  819.7 1.3 convolution_subtract_fusion.18
  821.3 1.4 convolution_subtract_fusion.17
  823.0 70.4 %psum.7 = f32[1024]{0:T(1024)S(1)} all-reduce(f32[1024]{0:T(1024)S(1)} %multiply_reduce_fusion), channel_id=1, replica_groups=mesh['dp'=32,'tensor'=4] {'dp','tensor'}, use_global_device_ids=true, to_apply=%region_19.20 | all-reduce | flops 1024 | bytes 8192 | tf_op jit(solution)/shard_map/psum | solution.py:38
  (95 shorter events, 21.3 us)
Async XLA Ops:
  7.4 92.3 %all-gather.2.cloned.1.call-start = ((), (), s32[]{:S(2)}) async-start(), calls=%async_computation.2 | async-start | bytes 2113536 | tf_op jit(solution)/shard_map/all_gather | solution.py:24
  8.1 152.6 %reduce-scatter.3.cloned.1.call-start = ((), (), s32[]{:S(2)}) async-start(), calls=%async_computation.3 | async-start | bytes 5242880 | tf_op jit(solution)/shard_map/reduce_scatter | solution.py:18
  21.9 779.3 %reduce-scatter.5.cloned.1.call-start = ((), (), s32[]{:S(2)}) async-start(), calls=%async_computation.4 | async-start | bytes 4227072 | tf_op jit(solution)/shard_map/reduce_scatter | solution.py:27
  104.2 2.0 copy-start
  118.9 2.0 copy-start.1
  120.8 39.9 %copy-start.2 = (bf16[1024,1024]{1,0:T(8,128)(2,1)S(1)}, bf16[1024,1024]{1,0:T(8,128)(2,1)}, u32[]{:S(2)}) copy-start(bf16[1024,1024]{1,0:T(8,128)(2,1)} %all-gather.2.cloned.1.call-done) | copy-start | bytes 6291460
Sparse Core Ops, SparseCore 0:
  11.2 88.4 all-gather.1
  166.7 634.4 reduce-scatter.4
Sparse Core Ops, SparseCore 1:
  22.0 50.3 reduce-scatter.2
where the time goes:
time: 908 us; the launch traced here: 902 us
  waiting for transfers between devices  444 us (49%)
  other arithmetic  263 us (29%)
  blocking collectives  70.4 us (8%)
  matrix products  68.9 us (8%)
  local copies, waits for them, and re-layouts  34.8 us (4%)
  between operations  20.4 us (2%)
    reduce_scatter x1, waiting for transfers between devices, shards(): lax.psum_scatter(lax.dot_general(summed, squared, (((0,), (0,)), ((), ())...  365 us
    another operation x30, other arithmetic, solve_rows(): lower = jnp.linalg.cholesky(hadamard)  172 us
    another operation x3, other arithmetic, solve_rows(): jax.scipy.linalg.solve_triangular(lower, first, lower=True, trans=1)  83.6 us
    all_gather x1, waiting for transfers between devices, shards(): whole_factor = lax.all_gather(factor, ('dp', 'tensor'), axis=0, tiled=True)  77.6 us
    psum x1, blocking collectives, shards(): lax.psum(jnp.sum(updated * updated, axis=0), ('dp', 'tensor'))  70.4 us
    another operation x14, matrix products, solve_rows(): lower = jnp.linalg.cholesky(hadamard)  23.3 us
    another operation x24, local copies, waits for them, and re-layouts  22.3 us
  transfers between devices with their start and end apart: 3, of which 2 were waited for; matrix products, arithmetic and copies ran while one was open for 37% of the time, Pallas kernels for 0%

commit v1 on v0

--- a/solution.py
+++ b/solution.py
@@ -21,7 +21,12 @@
         scatter_dimension=0,
         tiled=True,
     )
-    whole_factor = lax.all_gather(factor, ("dp", "tensor"), axis=0, tiled=True)
+    whole_factor = jnp.concatenate(
+        lax.all_to_all(
+            jnp.stack([factor] * lax.axis_size(("dp", "tensor"))), ("dp", "tensor"), 0, 0
+        ),
+        axis=0,
+    )
     projected = jnp.dot(summed, whole_factor, preferred_element_type=jnp.float32)
     squared = (projected * projected).astype(jnp.bfloat16)
     moment_rows = lax.psum_scatter(

time: 908 us -> 854 us (0.941)
  waiting for transfers between devices: 444 us -> 379 us
  starting transfers between devices: 0.09 us -> 11.6 us
    all_gather x1 -> x0, waiting for transfers between devices: 77.6 us -> none  [shards(): whole_factor = lax.all_gather(factor, ('dp', 'tensor'), axis=0, tiled=True)]
    all_to_all x0 -> x1, waiting for transfers between devices: none -> 17 us  [shards(): lax.all_to_all(jnp.stack([factor] * lax.axis_size(('dp', 'tensor'))), ('d...]
    all_to_all x0 -> x1, starting transfers between devices: none -> 11.5 us  [shards(): lax.all_to_all(jnp.stack([factor] * lax.axis_size(('dp', 'tensor'))), ('d...]
    another operation x24 -> x25, local copies, waits for them, and re-layouts: 22.3 us -> 24.6 us
  transfers between devices with their start and end apart: 3 -> 3, of which waited for: 2 -> 2; matrix products, arithmetic and copies ran while one was open for 37% -> 39% of each run, Pallas kernels for 0% -> 0%
where the time goes in v1:
time: 854 us; the launch traced here: 847 us
  waiting for transfers between devices  379 us (44%)
  other arithmetic  263 us (31%)
  blocking collectives  70.4 us (8%)
  matrix products  66.6 us (8%)
  local copies, waits for them, and re-layouts  37.2 us (4%)
  between operations  19 us (2%)
  starting transfers between devices  11.6 us (1%)
    reduce_scatter x1, waiting for transfers between devices, shards(): lax.psum_scatter(lax.dot_general(summed, squared, (((0,), (0,)), ((), ())...  362 us
    another operation x30, other arithmetic, solve_rows(): lower = jnp.linalg.cholesky(hadamard)  172 us
    another operation x3, other arithmetic, solve_rows(): jax.scipy.linalg.solve_triangular(lower, first, lower=True, trans=1)  83.7 us
    psum x1, blocking collectives, shards(): lax.psum(jnp.sum(updated * updated, axis=0), ('dp', 'tensor'))  70.4 us
    another operation x14, matrix products, solve_rows(): lower = jnp.linalg.cholesky(hadamard)  23.3 us
    another operation x24, local copies, waits for them, and re-layouts  22.3 us
  transfers between devices with their start and end apart: 3, of which 2 were waited for; matrix products, arithmetic and copies ran while one was open for 39% of the time, Pallas kernels for 0%

profile of v1, /device:TPU:1, one launch (start us, length us, event | category | flops | bytes accessed | tf_op | source)
XLA Modules:
  0.0 847.3 jit_solution(7015857367234878528)
XLA Ops:
  6.5 2.3 stack.2
  8.8 11.5 %all-to-all-start = ((bf16[128,8,1024]{2,1,0:T(8,128)(2,1)}), bf16[128,8,1024]{2,1,0:T(8,128)(2,1)S(1)}, u32[]{:S(2)}, u32[]{:S(2)}) async-start(bf16[128,8,1024]{2,1,0:T(8,128)(2,1)} %stack.2), calls=%async_computation | async-start | bytes 4194304 | tf_op jit(solution)/shard_map/all_to_all | solution.py:25
  20.4 13.8 %convolution_convert_fusion = bf16[2048,1024]{1,0:T(8,128)(2,1)} fusion(bf16[2048,2048]{1,0:T(8,128)(2,1)} %param.3, bf16[2048,1024]{1,0:T(8,128)(2,1)} %param.4), kind=kOutput, calls=%fused_computation.9 | convolution fusion | flops 8592031744 | bytes 16777216 | tf_op jit(solution)/shard_map/dot_general | solution.py:19
  34.2 17.0 %all-to-all-done = bf16[128,8,1024]{2,1,0:T(8,128)(2,1)S(1)} async-done(((bf16[128,8,1024]{2,1,0:T(8,128)(2,1)}), bf16[128,8,1024]{2,1,0:T(8,128)(2,1)S(1)}, u32[]{:S(2)}, u32[]{:S(2)}) %all-to-all-start) | async-done | bytes 2097184 | tf_op jit(solution)/shard_map/all_to_all | solution.py:25
  51.3 2.4 fusion.102
  53.7 2.0 copy-done
  55.6 2.4 fusion
  58.0 5.8 copy.11
  63.9 4.5 add_multiply_fusion
  68.4 2.0 copy-done.1
  70.4 11.7 %cholesky.222 = f32[128,128]{1,0:T(8,128)S(1)} custom-call(f32[128,128]{1,0:T(8,128)S(1)} %cholesky.577), custom_call_target="Cholesky" | custom-call | tf_op jit(solution)/shard_map/jit(cholesky)/cholesky | solution.py:11
  82.1 2.5 cholesky.254
  84.6 9.8 %custom-call.66 = f32[1,128,128]{1,2,0:T(8,128)S(1)} custom-call(f32[1,128,128]{2,1,0:T(8,128)S(1)} %get-tuple-element.44), custom_call_target="InvertDiagBlocksLowerTriangular" | custom-call | tf_op jit(solution)/shard_map/jit(cholesky)/cholesky | solution.py:11
  94.4 2.3 constant_dynamic-update-slice_fusion.50
  96.8 1.5 convolution_subtract_fusion
  98.3 11.9 %cholesky.243 = f32[128,128]{1,0:T(8,128)S(1)} custom-call(f32[128,128]{1,0:T(8,128)S(1)} %cholesky.581), custom_call_target="Cholesky" | custom-call | tf_op jit(solution)/shard_map/jit(cholesky)/cholesky | solution.py:11
  110.2 5.9 fusion.7
  116.8 9.8 %custom-call.67 = f32[1,128,128]{1,2,0:T(8,128)S(1)} custom-call(f32[1,128,128]{2,1,0:T(8,128)S(1)} %get-tuple-element.41), custom_call_target="InvertDiagBlocksLowerTriangular" | custom-call | tf_op jit(solution)/shard_map/jit(cholesky)/cholesky | solution.py:11
  126.6 1.2 convolution_dynamic-update-slice_fusion
  127.8 2.1 convolution_subtract_fusion.1
  130.0 11.7 %cholesky.466 = f32[128,128]{1,0:T(8,128)S(1)} custom-call(f32[128,128]{1,0:T(8,128)S(1)} %cholesky.586), custom_call_target="Cholesky" | custom-call | tf_op jit(solution)/shard_map/jit(cholesky)/cholesky | solution.py:11
  142.3 9.8 %custom-call.68 = f32[1,128,128]{1,2,0:T(8,128)S(1)} custom-call(f32[1,128,128]{2,1,0:T(8,128)S(1)} %get-tuple-element.38), custom_call_target="InvertDiagBlocksLowerTriangular" | custom-call | tf_op jit(solution)/shard_map/jit(cholesky)/cholesky | solution.py:11
  152.1 1.2 convolution_dynamic-update-slice_fusion.1
  153.3 2.5 convolution_subtract_fusion.2
  155.9 11.7 %cholesky.485 = f32[128,128]{1,0:T(8,128)S(1)} custom-call(f32[128,128]{1,0:T(8,128)S(1)} %cholesky.591), custom_call_target="Cholesky" | custom-call | tf_op jit(solution)/shard_map/jit(cholesky)/cholesky | solution.py:11
  168.2 9.8 %custom-call.69 = f32[1,128,128]{1,2,0:T(8,128)S(1)} custom-call(f32[1,128,128]{2,1,0:T(8,128)S(1)} %get-tuple-element.35), custom_call_target="InvertDiagBlocksLowerTriangular" | custom-call | tf_op jit(solution)/shard_map/jit(cholesky)/cholesky | solution.py:11
  178.0 1.1 convolution_dynamic-update-slice_fusion.2
  179.1 2.4 convolution_subtract_fusion.3
  181.5 11.7 %cholesky.504 = f32[128,128]{1,0:T(8,128)S(1)} custom-call(f32[128,128]{1,0:T(8,128)S(1)} %cholesky.596), custom_call_target="Cholesky" | custom-call | tf_op jit(solution)/shard_map/jit(cholesky)/cholesky | solution.py:11
  193.9 10.1 %custom-call.70 = f32[1,128,128]{1,2,0:T(8,128)S(1)} custom-call(f32[1,128,128]{2,1,0:T(8,128)S(1)} %get-tuple-element.32), custom_call_target="InvertDiagBlocksLowerTriangular" | custom-call | tf_op jit(solution)/shard_map/jit(cholesky)/cholesky | solution.py:11
  205.0 2.3 convolution_subtract_fusion.4
  207.3 11.7 %cholesky.524 = f32[128,128]{1,0:T(8,128)S(1)} custom-call(f32[128,128]{1,0:T(8,128)S(1)} %cholesky.601), custom_call_target="Cholesky" | custom-call | tf_op jit(solution)/shard_map/jit(cholesky)/cholesky | solution.py:11
  219.7 9.8 %custom-call.71 = f32[1,128,128]{1,2,0:T(8,128)S(1)} custom-call(f32[1,128,128]{2,1,0:T(8,128)S(1)} %get-tuple-element.29), custom_call_target="InvertDiagBlocksLowerTriangular" | custom-call | tf_op jit(solution)/shard_map/jit(cholesky)/cholesky | solution.py:11
  230.4 2.0 convolution_subtract_fusion.5
  232.5 11.9 %cholesky.544 = f32[128,128]{1,0:T(8,128)S(1)} custom-call(f32[128,128]{1,0:T(8,128)S(1)} %cholesky.606), custom_call_target="Cholesky" | custom-call | tf_op jit(solution)/shard_map/jit(cholesky)/cholesky | solution.py:11
  245.0 9.8 %custom-call.72 = f32[1,128,128]{1,2,0:T(8,128)S(1)} custom-call(f32[1,128,128]{2,1,0:T(8,128)S(1)} %get-tuple-element.26), custom_call_target="InvertDiagBlocksLowerTriangular" | custom-call | tf_op jit(solution)/shard_map/jit(cholesky)/cholesky | solution.py:11
  255.7 1.8 convolution_subtract_fusion.6
  257.5 11.7 %cholesky.562 = f32[128,128]{1,0:T(8,128)S(1)} custom-call(f32[128,128]{1,0:T(8,128)S(1)} %convolution_subtract_fusion.6), custom_call_target="Cholesky" | custom-call | tf_op jit(solution)/shard_map/jit(cholesky)/cholesky | solution.py:11
  279.3 4.9 select_select_fusion
  284.2 22.5 %while.1 = (s32[]{:T(128)}, f32[1024,1024]{1,0:T(8,128)}, s32[8,2]{0,1:T(2,128)S(1)}, f32[8,128,128]{2,1,0:T(8,128)S(1)}, s32[]{:T(128)}) while((s32[]{:T(128)}, f32[1024,1024]{1,0:T(8,128)}, s32[8,2]{0,1:T(2,128)S(1)}, f32[8,128,128]{2,1,0:T(8,128)S(1)}, s32[]{:T(128)}) %tuple.56), condition=%wide.while_cond, body=%wide.while_body.sunk | while | flops 2 | bytes 131189 | solution.py:13
  284.8 2.2 bitcast_dynamic-update-slice_fusion.2
  287.6 2.2 bitcast_dynamic-update-slice_fusion.2
  290.4 2.2 bitcast_dynamic-update-slice_fusion.2
  293.3 2.2 bitcast_dynamic-update-slice_fusion.2
  296.1 2.2 bitcast_dynamic-update-slice_fusion.2
  298.9 2.2 bitcast_dynamic-update-slice_fusion.2
  301.7 2.2 bitcast_dynamic-update-slice_fusion.2
  304.5 2.1 bitcast_dynamic-update-slice_fusion.2
  306.7 78.8 %custom-call.73 = f32[8,128,128]{1,2,0:T(8,128)S(1)} custom-call(f32[8,128,128]{2,1,0:T(8,128)S(1)} %get-tuple-element.12), custom_call_target="InvertDiagBlocksLowerTriangular" | custom-call | tf_op jit(solution)/shard_map/jit(_solve_triangular)/triangular_solve | solution.py:13
  385.5 362.2 %reduce-scatter.5.cloned.1.call-done = f32[8,1024]{1,0:T(8,128)} async-done(((f32[1024,1024]{1,0:T(8,128)}), f32[8,1024]{1,0:T(8,128)}) %reduce-scatter.5.cloned.1.call-update) | async-done | bytes 32784 | tf_op jit(solution)/shard_map/reduce_scatter | solution.py:32
  749.7 1.1 convolution_subtract_fusion.15
  751.0 1.2 convolution_subtract_fusion.14
  752.4 1.2 convolution_subtract_fusion.13
  753.9 1.4 convolution_subtract_fusion.12
  755.4 1.4 convolution_subtract_fusion.20
  757.0 1.5 convolution_subtract_fusion.19
  759.0 1.0 convolution_subtract_fusion.11
  760.2 1.1 convolution_subtract_fusion.10
  761.5 1.2 convolution_subtract_fusion.9
  762.9 1.2 convolution_subtract_fusion.8
  764.4 1.3 convolution_subtract_fusion.7
  765.9 1.3 convolution_subtract_fusion.18
  767.5 1.4 convolution_subtract_fusion.17
  769.2 70.4 %psum.7 = f32[1024]{0:T(1024)S(1)} all-reduce(f32[1024]{0:T(1024)S(1)} %multiply_reduce_fusion), channel_id=1, replica_groups=mesh['dp'=32,'tensor'=4] {'dp','tensor'}, use_global_device_ids=true, to_apply=%region_19.20 | all-reduce | flops 1024 | bytes 8192 | tf_op jit(solution)/shard_map/psum | solution.py:43
  (93 shorter events, 22.5 us)
Async XLA Ops:
  8.8 42.4 %all-to-all-start = ((bf16[128,8,1024]{2,1,0:T(8,128)(2,1)}), bf16[128,8,1024]{2,1,0:T(8,128)(2,1)S(1)}, u32[]{:S(2)}, u32[]{:S(2)}) async-start(bf16[128,8,1024]{2,1,0:T(8,128)(2,1)} %stack.2), calls=%async_computation | async-start | bytes 4194304 | tf_op jit(solution)/shard_map/all_to_all | solution.py:25
  20.3 89.9 %reduce-scatter.3.cloned.1.call-start = ((), (), s32[]{:S(2)}) async-start(), calls=%async_computation.3 | async-start | bytes 5242880 | tf_op jit(solution)/shard_map/reduce_scatter | solution.py:18
  34.2 713.5 %reduce-scatter.5.cloned.1.call-start = ((), (), s32[]{:S(2)}) async-start(), calls=%async_computation.4 | async-start | bytes 4227072 | tf_op jit(solution)/shard_map/reduce_scatter | solution.py:32
  53.6 2.0 copy-start
  68.4 2.0 copy-start.1
Sparse Core Ops, SparseCore 0:
  34.3 49.8 reduce-scatter.2
  116.2 631.3 reduce-scatter.4
